TPU v7x, 512 devices: a whole 4x8x8 slice. The times are simulated.
512 devices in a mesh: dp: 4 (over y_lo), seq: 32 (over z, y_hi, core), tensor: 4 (over x).
Axes of the slice: x: 4, y: 8 (y_hi: 2, y_lo: 4; y = y_hi * 4 + y_lo), z: 8, core: 2. Of those that a mesh axis runs over, the one named last changes fastest.
Arguments:
- queries: bfloat16 [4, 16384, 512], P('dp', 'seq', 'tensor'), may hold values from -6 to 6
- values: bfloat16 [4, 16384, 512], P('dp', 'seq', 'tensor'), may hold values from -6 to 6
- filt: float32 [16384, 512], P('seq', 'tensor'), may hold values from -4 to 4
- w_out: bfloat16 [512, 4096], P('tensor'), may hold values from -0.375 to 0.375
- cotangent: bfloat16 [4, 16384, 4096], P('dp', 'seq', 'tensor'), may hold values from -6 to 6
Outputs:
- mixed: bfloat16 [4, 16384, 4096], P('dp', 'seq', 'tensor')
- grad_query: bfloat16 [4, 16384, 512], P('dp', 'seq', 'tensor')
- grad_value: bfloat16 [4, 16384, 512], P('dp', 'seq', 'tensor')
- grad_filt: float32 [16384, 512], P('seq', 'tensor')
All inputs are finite; a program needn't handle non-finite values.
Results may differ from a plain program's by a relative error of at most 0.024.
Values may be sent and summed in bfloat16 or wider, within the bound.
No kernel may reach another device: no remote copies, remote signals or barrier semaphores. Data moves between devices by JAX's collectives and lax.ppermute only.
A program may use at most 64 MiB of HBM per device.

v0:
```python
import math
import jax
import jax.numpy as jnp
from jax import lax
from jax.sharding import PartitionSpec as P

HIGHEST = lax.Precision.HIGHEST


def for_sending(array):
    return jax.tree.map(lambda a: a.astype(jnp.bfloat16) if a.dtype == jnp.float32 else a, array)


def angle_table(first, second, period):
    index = first[:, None] * second[None, :] % period
    angle = -2.0 * math.pi / period * index.astype(jnp.float32)
    return (jnp.cos(angle), jnp.sin(angle))


def product(table_real, table_imag, data_real, data_imag, form):

    def apply(left, right):
        return jnp.einsum(form, left, right, precision=HIGHEST)

    return (
        apply(table_real, data_real) - apply(table_imag, data_imag),
        apply(table_real, data_imag) + apply(table_imag, data_real),
    )


def split_length(length):
    levels = length.bit_length() - 1
    inner = 1 << levels // 2
    return (inner, length // inner)


def local_forward(data_real, data_imag, freq_index, total):
    pair, length, width = data_real.shape
    inner, outer = split_length(length)
    cos_t, sin_t = angle_table(freq_index, jnp.arange(length, dtype=jnp.int32), total)
    cos_t = cos_t[:, :, None]
    sin_t = sin_t[:, :, None]
    data_real, data_imag = (
        data_real * cos_t - data_imag * sin_t,
        data_real * sin_t + data_imag * cos_t,
    )
    data_real = data_real.reshape(pair, outer, inner, width)
    data_imag = data_imag.reshape(pair, outer, inner, width)
    outer_c, outer_s = angle_table(
        jnp.arange(outer, dtype=jnp.int32), jnp.arange(outer, dtype=jnp.int32), outer
    )
    data_real, data_imag = product(outer_c, outer_s, data_real, data_imag, "ab,ebcd->eacd")
    mid_c, mid_s = angle_table(
        jnp.arange(outer, dtype=jnp.int32), jnp.arange(inner, dtype=jnp.int32), length
    )
    mid_c = mid_c[None, :, :, None]
    mid_s = mid_s[None, :, :, None]
    data_real, data_imag = (
        data_real * mid_c - data_imag * mid_s,
        data_real * mid_s + data_imag * mid_c,
    )
    inner_c, inner_s = angle_table(
        jnp.arange(inner, dtype=jnp.int32), jnp.arange(inner, dtype=jnp.int32), inner
    )
    return product(inner_c, inner_s, data_real, data_imag, "ab,ecbd->ecad")


def local_inverse(spec_real, spec_imag, freq_index, total):
    pair, outer, inner, width = spec_real.shape
    length = outer * inner
    inner_c, inner_s = angle_table(
        jnp.arange(inner, dtype=jnp.int32), jnp.arange(inner, dtype=jnp.int32), inner
    )
    data_real, data_imag = product(
        inner_c / inner, -inner_s / inner, spec_real, spec_imag, "ab,ecbd->ecad"
    )
    mid_c, mid_s = angle_table(
        jnp.arange(outer, dtype=jnp.int32), jnp.arange(inner, dtype=jnp.int32), length
    )
    mid_c = mid_c[None, :, :, None]
    mid_s = mid_s[None, :, :, None]
    data_real, data_imag = (
        data_real * mid_c + data_imag * mid_s,
        data_imag * mid_c - data_real * mid_s,
    )
    outer_c, outer_s = angle_table(
        jnp.arange(outer, dtype=jnp.int32), jnp.arange(outer, dtype=jnp.int32), outer
    )
    data_real, data_imag = product(
        outer_c / outer, -outer_s / outer, data_real, data_imag, "ab,ebcd->eacd"
    )
    data_real = data_real.reshape(pair, length, width)
    data_imag = data_imag.reshape(pair, length, width)
    cos_t, sin_t = angle_table(freq_index, jnp.arange(length, dtype=jnp.int32), total)
    cos_t = cos_t[:, :, None]
    sin_t = sin_t[:, :, None]
    return (data_real * cos_t + data_imag * sin_t, data_imag * cos_t - data_real * sin_t)


def forward_transform(signal):
    count = lax.axis_size("seq")
    place = lax.axis_index("seq")
    length, width = signal.shape
    total = 2 * count * length
    pieces = lax.all_to_all(
        signal.reshape(count, length // count, width).astype(jnp.bfloat16),
        "seq",
        split_axis=0,
        concat_axis=0,
        tiled=True,
    ).astype(jnp.float32)
    cos_t, sin_t = angle_table(
        jnp.arange(2 * count, dtype=jnp.int32), jnp.arange(count, dtype=jnp.int32), 2 * count
    )
    mixed_real = jnp.einsum("ka,arc->krc", cos_t, pieces, precision=HIGHEST)
    mixed_imag = jnp.einsum("ka,arc->krc", sin_t, pieces, precision=HIGHEST)
    mixed_real, mixed_imag = (
        lax.all_to_all(
            for_sending(mixed_real), "seq", split_axis=0, concat_axis=1, tiled=True
        ).astype(mixed_real.dtype),
        lax.all_to_all(
            for_sending(mixed_imag), "seq", split_axis=0, concat_axis=1, tiled=True
        ).astype(mixed_imag.dtype),
    )
    freq_index = 2 * place + jnp.arange(2, dtype=jnp.int32)
    return (local_forward(mixed_real, mixed_imag, freq_index, total), freq_index)


def inverse_transform(spectrum, freq_index):
    count = lax.axis_size("seq")
    pair, outer, inner, width = spectrum[0].shape
    length = outer * inner
    total = 2 * count * length
    data_real, data_imag = local_inverse(spectrum[0], spectrum[1], freq_index, total)
    part_real, part_imag = (
        lax.all_to_all(
            for_sending(data_real), "seq", split_axis=1, concat_axis=0, tiled=True
        ).astype(data_real.dtype),
        lax.all_to_all(
            for_sending(data_imag), "seq", split_axis=1, concat_axis=0, tiled=True
        ).astype(data_imag.dtype),
    )
    cos_t, sin_t = angle_table(
        jnp.arange(2 * count, dtype=jnp.int32), jnp.arange(count, dtype=jnp.int32), 2 * count
    )
    signal = (
        jnp.einsum("ka,krc->arc", cos_t, part_real, precision=HIGHEST)
        + jnp.einsum("ka,krc->arc", sin_t, part_imag, precision=HIGHEST)
    ) / (2 * count)
    signal = lax.all_to_all(
        for_sending(signal), "seq", split_axis=0, concat_axis=0, tiled=True
    ).astype(signal.dtype)
    return signal.reshape(length, width)


def split_spec(spectrum, width):
    first = (spectrum[0][..., :width], spectrum[1][..., :width])
    second = (spectrum[0][..., width:], spectrum[1][..., width:])
    return (first, second)


def times_spec(left, right):
    return (left[0] * right[0] - left[1] * right[1], left[0] * right[1] + left[1] * right[0])


def conj_times(left, right):
    return (left[0] * right[0] + left[1] * right[1], left[0] * right[1] - left[1] * right[0])


def per_device(queries, values, filt, w_out, cotangent):
    query = queries[0].astype(jnp.float32)
    value = values[0].astype(jnp.float32)
    width = filt.shape[1]
    joined = jnp.concatenate([value, filt], axis=1)
    spectrum, freq_index = forward_transform(joined)
    value_spec, filt_spec = split_spec(spectrum, width)
    conv = inverse_transform(times_spec(value_spec, filt_spec), freq_index)
    gated = (query * conv).astype(jnp.bfloat16)
    partial_sum = jnp.dot(gated, w_out, preferred_element_type=jnp.float32)
    mixed = lax.psum_scatter(
        partial_sum.astype(jnp.bfloat16), "tensor", scatter_dimension=1, tiled=True
    )
    grad_gated = lax.dot_general(
        lax.all_gather(cotangent[0], "tensor", axis=1, tiled=True),
        w_out,
        (((1,), (1,)), ((), ())),
        preferred_element_type=jnp.float32,
    )
    grad_query = (grad_gated * conv).astype(jnp.bfloat16)
    grad_conv = grad_gated * query
    grad_spec = forward_transform(grad_conv)[0]
    back_value = conj_times(filt_spec, grad_spec)
    back_filt = conj_times(value_spec, grad_spec)
    both_spec = (
        jnp.concatenate([back_value[0], back_filt[0]], axis=3),
        jnp.concatenate([back_value[1], back_filt[1]], axis=3),
    )
    result = inverse_transform(both_spec, freq_index)
    grad_value = result[:, :width].astype(jnp.bfloat16)
    grad_filt = lax.psum(result[:, width:].astype(jnp.bfloat16), "dp").astype(jnp.float32)
    return (mixed[None], grad_query[None], grad_value[None], grad_filt)


def solution(mesh):
    placed = (
        P("dp", "seq", "tensor"),
        P("dp", "seq", "tensor"),
        P("seq", "tensor"),
        P("tensor", None),
        P("dp", "seq", "tensor"),
    )
    return jax.shard_map(
        per_device,
        mesh=mesh,
        in_specs=placed,
        out_specs=(
            P("dp", "seq", "tensor"),
            P("dp", "seq", "tensor"),
            P("dp", "seq", "tensor"),
            P("seq", "tensor"),
        ),
        check_vma=False,
    )
```

profile of v0, /device:TPU:1, one launch (start us, length us, event | category | flops | bytes accessed | tf_op | source)
XLA Modules:
  0.0 429.1 jit_solution(16543263097162809174)
XLA Ops:
  9.8 30.7 %all_to_all.128 = bf16[32,16,256]{2,1,0:T(8,128)(2,1)S(1)} all-to-all(bf16[32,16,256]{2,1,0:T(8,128)(2,1)S(1)} %bitcast.303), channel_id=1, replica_groups=mesh['dp'=4,'seq'=32,'tensor'=4] {'seq'}, dimensions={0} | all-to-all | bytes 524288 | tf_op jit(solution)/shard_map/all_to_all | solution.py:105
  42.3 5.8 %all-to-all-start.1 = ((bf16[64,16,256]{2,1,0:T(8,128)(2,1)}), bf16[64,16,256]{2,1,0:T(8,128)(2,1)S(1)}, u32[]{:S(2)}, u32[]{:S(2)}) async-start(bf16[64,16,256]{2,1,0:T(8,128)(2,1)} %copy.71), calls=%async_computation.1 | async-start | bytes 1048576 | tf_op jit(solution)/shard_map/all_to_all | solution.py:118
  49.9 14.1 %all-to-all-done.1 = bf16[64,16,256]{2,1,0:T(8,128)(2,1)S(1)} async-done(((bf16[64,16,256]{2,1,0:T(8,128)(2,1)}), bf16[64,16,256]{2,1,0:T(8,128)(2,1)S(1)}, u32[]{:S(2)}, u32[]{:S(2)}) %all-to-all-start.1) | async-done | bytes 524320 | tf_op jit(solution)/shard_map/all_to_all | solution.py:118
  64.0 9.6 %all-to-all-start.2 = ((bf16[64,16,256]{2,1,0:T(8,128)(2,1)}), bf16[64,16,256]{2,1,0:T(8,128)(2,1)}, u32[]{:S(2)}, u32[]{:S(2)}) async-start(bf16[64,16,256]{2,1,0:T(8,128)(2,1)} %copy.74), calls=%async_computation.2 | async-start | bytes 1048576 | tf_op jit(solution)/shard_map/all_to_all | solution.py:121
  74.3 15.0 %all-to-all-done.2 = bf16[64,16,256]{2,1,0:T(8,128)(2,1)} async-done(((bf16[64,16,256]{2,1,0:T(8,128)(2,1)}), bf16[64,16,256]{2,1,0:T(8,128)(2,1)}, u32[]{:S(2)}, u32[]{:S(2)}) %all-to-all-start.2) | async-done | bytes 524320 | tf_op jit(solution)/shard_map/all_to_all | solution.py:121
  105.8 9.8 %all-to-all-start.6 = ((bf16[32,16,128]{2,1,0:T(8,128)(2,1)}), bf16[32,16,128]{2,1,0:T(8,128)(2,1)S(1)}, u32[]{:S(2)}, u32[]{:S(2)}) async-start(bf16[32,16,128]{2,1,0:T(8,128)(2,1)} %bitcast.55), calls=%async_computation.7 | async-start | bytes 262144 | tf_op jit(solution)/shard_map/all_to_all | solution.py:105
  118.2 9.6 %all-to-all-done.6 = bf16[32,16,128]{2,1,0:T(8,128)(2,1)S(1)} async-done(((bf16[32,16,128]{2,1,0:T(8,128)(2,1)}), bf16[32,16,128]{2,1,0:T(8,128)(2,1)S(1)}, u32[]{:S(2)}, u32[]{:S(2)}) %all-to-all-start.6) | async-done | bytes 131104 | tf_op jit(solution)/shard_map/all_to_all | solution.py:105
  139.1 8.6 %all-to-all-done.7 = bf16[64,16,128]{2,1,0:T(8,128)(2,1)} async-done(((bf16[64,16,128]{2,1,0:T(8,128)(2,1)}), bf16[64,16,128]{2,1,0:T(8,128)(2,1)}, u32[]{:S(2)}, u32[]{:S(2)}) %all-to-all-start.7) | async-done | bytes 262176 | tf_op jit(solution)/shard_map/all_to_all | solution.py:118
  147.7 5.8 %all-to-all-start.8 = ((bf16[64,16,128]{2,1,0:T(8,128)(2,1)}), bf16[64,16,128]{2,1,0:T(8,128)(2,1)S(1)}, u32[]{:S(2)}, u32[]{:S(2)}) async-start(bf16[64,16,128]{2,1,0:T(8,128)(2,1)} %copy.99), calls=%async_computation.9 | async-start | bytes 524288 | tf_op jit(solution)/shard_map/all_to_all | solution.py:121
  157.8 9.4 %all-to-all-done.8 = bf16[64,16,128]{2,1,0:T(8,128)(2,1)S(1)} async-done(((bf16[64,16,128]{2,1,0:T(8,128)(2,1)}), bf16[64,16,128]{2,1,0:T(8,128)(2,1)S(1)}, u32[]{:S(2)}, u32[]{:S(2)}) %all-to-all-start.8) | async-done | bytes 262176 | tf_op jit(solution)/shard_map/all_to_all | solution.py:121
  192.9 5.8 %all-to-all-start.10 = ((bf16[2,512,256]{2,0,1:T(2,128)(2,1)}), bf16[2,512,256]{2,0,1:T(2,128)(2,1)S(1)}, u32[]{:S(2)}, u32[]{:S(2)}) async-start(bf16[2,512,256]{2,0,1:T(2,128)(2,1)} %copy.116), calls=%async_computation.11 | async-start | bytes 1048576 | tf_op jit(solution)/shard_map/all_to_all | solution.py:139
  203.8 10.6 %all-to-all-done.10 = bf16[2,512,256]{2,0,1:T(2,128)(2,1)S(1)} async-done(((bf16[2,512,256]{2,0,1:T(2,128)(2,1)}), bf16[2,512,256]{2,0,1:T(2,128)(2,1)S(1)}, u32[]{:S(2)}, u32[]{:S(2)}) %all-to-all-start.10) | async-done | bytes 524320 | tf_op jit(solution)/shard_map/all_to_all | solution.py:139
  214.5 9.3 %all-to-all-start.9 = ((bf16[2,512,256]{2,0,1:T(2,128)(2,1)}), bf16[2,512,256]{2,0,1:T(2,128)(2,1)}, u32[]{:S(2)}, u32[]{:S(2)}) async-start(bf16[2,512,256]{2,0,1:T(2,128)(2,1)} %copy.113), calls=%async_computation.10 | async-start | bytes 1048576 | tf_op jit(solution)/shard_map/all_to_all | solution.py:136
  228.1 11.6 %all-to-all-done.9 = bf16[2,512,256]{2,0,1:T(2,128)(2,1)} async-done(((bf16[2,512,256]{2,0,1:T(2,128)(2,1)}), bf16[2,512,256]{2,0,1:T(2,128)(2,1)}, u32[]{:S(2)}, u32[]{:S(2)}) %all-to-all-start.9) | async-done | bytes 524320 | tf_op jit(solution)/shard_map/all_to_all | solution.py:136
  239.7 9.6 %all-to-all-start.4 = ((bf16[2,512,128]{2,0,1:T(2,128)(2,1)}), bf16[2,512,128]{2,0,1:T(2,128)(2,1)S(1)}, u32[]{:S(2)}, u32[]{:S(2)}) async-start(bf16[2,512,128]{2,0,1:T(2,128)(2,1)} %copy.91), calls=%async_computation.4 | async-start | bytes 524288 | tf_op jit(solution)/shard_map/all_to_all | solution.py:139
  253.0 9.8 %all-to-all-done.4 = bf16[2,512,128]{2,0,1:T(2,128)(2,1)S(1)} async-done(((bf16[2,512,128]{2,0,1:T(2,128)(2,1)}), bf16[2,512,128]{2,0,1:T(2,128)(2,1)S(1)}, u32[]{:S(2)}, u32[]{:S(2)}) %all-to-all-start.4) | async-done | bytes 262176 | tf_op jit(solution)/shard_map/all_to_all | solution.py:139
  262.8 5.8 %all-to-all-start.3 = ((bf16[2,512,128]{2,0,1:T(2,128)(2,1)}), bf16[2,512,128]{2,0,1:T(2,128)(2,1)S(1)}, u32[]{:S(2)}, u32[]{:S(2)}) async-start(bf16[2,512,128]{2,0,1:T(2,128)(2,1)} %copy.88), calls=%async_computation.3 | async-start | bytes 524288 | tf_op jit(solution)/shard_map/all_to_all | solution.py:136
  270.4 11.9 %all-to-all-done.3 = bf16[2,512,128]{2,0,1:T(2,128)(2,1)S(1)} async-done(((bf16[2,512,128]{2,0,1:T(2,128)(2,1)}), bf16[2,512,128]{2,0,1:T(2,128)(2,1)S(1)}, u32[]{:S(2)}, u32[]{:S(2)}) %all-to-all-start.3) | async-done | bytes 262176 | tf_op jit(solution)/shard_map/all_to_all | solution.py:136
  282.3 5.8 %all-to-all-start.11 = ((bf16[32,16,256]{2,1,0:T(8,128)(2,1)}), bf16[32,16,256]{2,1,0:T(8,128)(2,1)S(1)}, u32[]{:S(2)}, u32[]{:S(2)}) async-start(bf16[32,16,256]{2,1,0:T(8,128)(2,1)} %copy.119), calls=%async_computation.12 | async-start | bytes 524288 | tf_op jit(solution)/shard_map/all_to_all | solution.py:150
  290.2 11.6 %all-to-all-done.11 = bf16[32,16,256]{2,1,0:T(8,128)(2,1)S(1)} async-done(((bf16[32,16,256]{2,1,0:T(8,128)(2,1)}), bf16[32,16,256]{2,1,0:T(8,128)(2,1)S(1)}, u32[]{:S(2)}, u32[]{:S(2)}) %all-to-all-start.11) | async-done | bytes 262176 | tf_op jit(solution)/shard_map/all_to_all | solution.py:150
  301.8 5.8 %all-to-all-start.5 = ((bf16[32,16,128]{2,1,0:T(8,128)(2,1)}), bf16[32,16,128]{2,1,0:T(8,128)(2,1)S(1)}, u32[]{:S(2)}, u32[]{:S(2)}) async-start(bf16[32,16,128]{2,1,0:T(8,128)(2,1)} %copy.94), calls=%async_computation.5 | async-start | bytes 262144 | tf_op jit(solution)/shard_map/all_to_all | solution.py:150
  308.4 11.5 %all-to-all-done.5 = bf16[32,16,128]{2,1,0:T(8,128)(2,1)S(1)} async-done(((bf16[32,16,128]{2,1,0:T(8,128)(2,1)}), bf16[32,16,128]{2,1,0:T(8,128)(2,1)S(1)}, u32[]{:S(2)}, u32[]{:S(2)}) %all-to-all-start.5) | async-done | bytes 131104 | tf_op jit(solution)/shard_map/all_to_all | solution.py:150
  323.9 41.7 %all-reduce.2.cloned.1.call-done = bf16[512,128]{1,0:T(8,128)(2,1)} async-done(((bf16[512,128]{1,0:T(8,128)(2,1)}), bf16[512,128]{1,0:T(8,128)(2,1)}) %all-reduce.2.cloned.1.call-update) | async-done | bytes 131088 | tf_op jit(solution)/shard_map/psum | solution.py:200
  367.3 55.0 %reduce-scatter.2.cloned.1.call-done = bf16[512,1024]{1,0:T(8,128)(2,1)} async-done(((bf16[512,4096]{1,0:T(8,128)(2,1)}), bf16[512,1024]{1,0:T(8,128)(2,1)}) %reduce-scatter.2.cloned.1.call-update) | async-done | bytes 1048592 | tf_op jit(solution)/shard_map/reduce_scatter | solution.py:180
  (104 shorter events, 90.1 us)
Async XLA Ops:
  7.2 94.4 %copy-start = (bf16[128,4096]{1,0:T(8,128)(2,1)S(1)}, bf16[128,4096]{1,0:T(8,128)(2,1)}, u32[]{:S(2)}) copy-start(bf16[128,4096]{1,0:T(8,128)(2,1)} %param.8) | copy-start | bytes 3145732
  7.2 94.3 %all-gather.3.cloned.1.call-start = ((), (), s32[]{:S(2)}) async-start(), calls=%async_computation.15 | async-start | bytes 5242880 | tf_op jit(solution)/shard_map/all_gather | solution.py:184
  42.3 21.7 %all-to-all-start.1 = ((bf16[64,16,256]{2,1,0:T(8,128)(2,1)}), bf16[64,16,256]{2,1,0:T(8,128)(2,1)S(1)}, u32[]{:S(2)}, u32[]{:S(2)}) async-start(bf16[64,16,256]{2,1,0:T(8,128)(2,1)} %copy.71), calls=%async_computation.1 | async-start | bytes 1048576 | tf_op jit(solution)/shard_map/all_to_all | solution.py:118
  64.0 25.3 %all-to-all-start.2 = ((bf16[64,16,256]{2,1,0:T(8,128)(2,1)}), bf16[64,16,256]{2,1,0:T(8,128)(2,1)}, u32[]{:S(2)}, u32[]{:S(2)}) async-start(bf16[64,16,256]{2,1,0:T(8,128)(2,1)} %copy.74), calls=%async_computation.2 | async-start | bytes 1048576 | tf_op jit(solution)/shard_map/all_to_all | solution.py:121
  97.7 3.9 copy-start.4
  101.5 32.4 %copy-start.1 = (f32[2,32,16,256]{3,1,2,0:T(8,128)S(1)}, f32[2,32,16,256]{3,1,2,0:T(8,128)}, u32[]{:S(2)}) copy-start(f32[2,32,16,256]{3,1,2,0:T(8,128)} %get-tuple-element.11) | copy-start | bytes 3145732
  105.8 22.0 %all-to-all-start.6 = ((bf16[32,16,128]{2,1,0:T(8,128)(2,1)}), bf16[32,16,128]{2,1,0:T(8,128)(2,1)S(1)}, u32[]{:S(2)}, u32[]{:S(2)}) async-start(bf16[32,16,128]{2,1,0:T(8,128)(2,1)} %bitcast.55), calls=%async_computation.7 | async-start | bytes 262144 | tf_op jit(solution)/shard_map/all_to_all | solution.py:105
  129.2 18.4 %all-to-all-start.7 = ((bf16[64,16,128]{2,1,0:T(8,128)(2,1)}), bf16[64,16,128]{2,1,0:T(8,128)(2,1)}, u32[]{:S(2)}, u32[]{:S(2)}) async-start(bf16[64,16,128]{2,1,0:T(8,128)(2,1)} %copy.96), calls=%async_computation.8 | async-start | bytes 524288 | tf_op jit(solution)/shard_map/all_to_all | solution.py:118
  147.7 19.5 %all-to-all-start.8 = ((bf16[64,16,128]{2,1,0:T(8,128)(2,1)}), bf16[64,16,128]{2,1,0:T(8,128)(2,1)S(1)}, u32[]{:S(2)}, u32[]{:S(2)}) async-start(bf16[64,16,128]{2,1,0:T(8,128)(2,1)} %copy.99), calls=%async_computation.9 | async-start | bytes 524288 | tf_op jit(solution)/shard_map/all_to_all | solution.py:121
  169.8 5.5 %copy-start.2 = (f32[2,32,16,256]{3,2,1,0:T(8,128)S(1)}, f32[2,32,16,256]{3,2,1,0:T(8,128)}, u32[]{:S(2)}) copy-start(f32[2,32,16,256]{3,2,1,0:T(8,128)} %fusion.5) | copy-start | bytes 3145732
  192.9 21.6 %all-to-all-start.10 = ((bf16[2,512,256]{2,0,1:T(2,128)(2,1)}), bf16[2,512,256]{2,0,1:T(2,128)(2,1)S(1)}, u32[]{:S(2)}, u32[]{:S(2)}) async-start(bf16[2,512,256]{2,0,1:T(2,128)(2,1)} %copy.116), calls=%async_computation.11 | async-start | bytes 1048576 | tf_op jit(solution)/shard_map/all_to_all | solution.py:139
  214.5 25.2 %all-to-all-start.9 = ((bf16[2,512,256]{2,0,1:T(2,128)(2,1)}), bf16[2,512,256]{2,0,1:T(2,128)(2,1)}, u32[]{:S(2)}, u32[]{:S(2)}) async-start(bf16[2,512,256]{2,0,1:T(2,128)(2,1)} %copy.113), calls=%async_computation.10 | async-start | bytes 1048576 | tf_op jit(solution)/shard_map/all_to_all | solution.py:136
  239.7 23.1 %all-to-all-start.4 = ((bf16[2,512,128]{2,0,1:T(2,128)(2,1)}), bf16[2,512,128]{2,0,1:T(2,128)(2,1)S(1)}, u32[]{:S(2)}, u32[]{:S(2)}) async-start(bf16[2,512,128]{2,0,1:T(2,128)(2,1)} %copy.91), calls=%async_computation.4 | async-start | bytes 524288 | tf_op jit(solution)/shard_map/all_to_all | solution.py:139
  253.0 67.0 %copy-start.5 = (bf16[1,512,128]{2,1,0:T(8,128)(2,1)S(1)}, bf16[1,512,128]{2,1,0:T(8,128)(2,1)}, u32[]{:S(2)}) copy-start(bf16[1,512,128]{2,1,0:T(8,128)(2,1)} %param.5) | copy-start | bytes 393220
  262.8 19.5 %all-to-all-start.3 = ((bf16[2,512,128]{2,0,1:T(2,128)(2,1)}), bf16[2,512,128]{2,0,1:T(2,128)(2,1)S(1)}, u32[]{:S(2)}, u32[]{:S(2)}) async-start(bf16[2,512,128]{2,0,1:T(2,128)(2,1)} %copy.88), calls=%async_computation.3 | async-start | bytes 524288 | tf_op jit(solution)/shard_map/all_to_all | solution.py:136
  282.3 19.5 %all-to-all-start.11 = ((bf16[32,16,256]{2,1,0:T(8,128)(2,1)}), bf16[32,16,256]{2,1,0:T(8,128)(2,1)S(1)}, u32[]{:S(2)}, u32[]{:S(2)}) async-start(bf16[32,16,256]{2,1,0:T(8,128)(2,1)} %copy.119), calls=%async_computation.12 | async-start | bytes 524288 | tf_op jit(solution)/shard_map/all_to_all | solution.py:150
  301.8 18.2 %all-to-all-start.5 = ((bf16[32,16,128]{2,1,0:T(8,128)(2,1)}), bf16[32,16,128]{2,1,0:T(8,128)(2,1)S(1)}, u32[]{:S(2)}, u32[]{:S(2)}) async-start(bf16[32,16,128]{2,1,0:T(8,128)(2,1)} %copy.94), calls=%async_computation.5 | async-start | bytes 262144 | tf_op jit(solution)/shard_map/all_to_all | solution.py:150
  307.6 58.1 %all-reduce.2.cloned.1.call-start = ((), (), s32[]{:S(2)}) async-start(), calls=%async_computation.14 | async-start | bytes 262144 | tf_op jit(solution)/shard_map/psum | solution.py:200
  308.4 113.9 %reduce-scatter.2.cloned.1.call-start = ((), (), s32[]{:S(2)}) async-start(), calls=%async_computation.13 | async-start | bytes 5242880 | tf_op jit(solution)/shard_map/reduce_scatter | solution.py:180
  320.0 3.3 copy-start.3
Sparse Core Ops, SparseCore 0:
  10.1 59.0 all-gather.2
  311.4 54.2 all-reduce.1
  369.3 52.8 reduce-scatter.1
where the time goes:
time: 433 us; the launch traced here: 429 us
  waiting for transfers between devices  221 us (51%)
  starting transfers between devices  78.1 us (18%)
  matrix products  59 us (14%)
  blocking collectives  30.7 us (7%)
  local copies, waits for them, and re-layouts  17.2 us (4%)
  between operations  14.6 us (3%)
  other arithmetic  8.43 us (2%)
    reduce_scatter x1, waiting for transfers between devices, per_device(): lax.psum_scatter(partial_sum.astype(jnp.bfloat16), 'tensor', scatter_dime...  55 us
    dot_general x32, matrix products, apply(): return jnp.einsum(form, left, right, precision=HIGHEST)  47.5 us
    psum x1, waiting for transfers between devices, per_device(): lax.psum(result[:, width:].astype(jnp.bfloat16), 'dp').astype(jnp.float32)  41.7 us
    all_to_all x1, blocking collectives, forward_transform(): lax.all_to_all(signal.reshape(count, length // count, width).astype(jnp.b...  30.7 us
    all_to_all x2, waiting for transfers between devices, forward_transform(): lax.all_to_all(for_sending(mixed_imag), 'seq', split_axis=0, concat_axis=...  24.4 us
    all_to_all x2, waiting for transfers between devices, inverse_transform(): lax.all_to_all(for_sending(data_real), 'seq', split_axis=1, concat_axis=0...  23.5 us
    all_to_all x2, waiting for transfers between devices, inverse_transform(): lax.all_to_all(for_sending(signal), 'seq', split_axis=0, concat_axis=0, t...  23.1 us
    all_to_all x2, waiting for transfers between devices, forward_transform(): lax.all_to_all(for_sending(mixed_real), 'seq', split_axis=0, concat_axis=...  22.7 us
  transfers between devices with their start and end apart: 14, of which 13 were waited for; matrix products, arithmetic and copies ran while one was open for 12% of the time, Pallas kernels for 0%

commit v1 on v0

--- a/solution.py
+++ b/solution.py
@@ -1,3 +1,4 @@
+import functools
 import math
 import jax
 import jax.numpy as jnp
@@ -5,6 +6,22 @@
 from jax.sharding import PartitionSpec as P
 
 HIGHEST = lax.Precision.HIGHEST
+
+
+def update_the_cells(m, which_dim, dim_k):
+    base_arr = jnp.concatenate(
+        lax.all_to_all(
+            jnp.stack(jnp.split(m, lax.axis_size("seq"), axis=which_dim)),
+            axis_name="seq",
+            split_axis=0,
+            concat_axis=0,
+        ),
+        axis=dim_k,
+    )
+    return base_arr
+
+
+layers_all_load = functools.partial(update_the_cells, which_dim=0, dim_k=1)
 
 
 def for_sending(array):
@@ -115,9 +132,7 @@
     mixed_real = jnp.einsum("ka,arc->krc", cos_t, pieces, precision=HIGHEST)
     mixed_imag = jnp.einsum("ka,arc->krc", sin_t, pieces, precision=HIGHEST)
     mixed_real, mixed_imag = (
-        lax.all_to_all(
-            for_sending(mixed_real), "seq", split_axis=0, concat_axis=1, tiled=True
-        ).astype(mixed_real.dtype),
+        layers_all_load(for_sending(mixed_real)).astype(mixed_real.dtype),
         lax.all_to_all(
             for_sending(mixed_imag), "seq", split_axis=0, concat_axis=1, tiled=True
         ).astype(mixed_imag.dtype),

time: 433 us -> 456 us (1.053)
  local copies, waits for them, and re-layouts: 17.2 us -> 55.2 us
  blocking collectives: 30.7 us -> 0 us
  starting transfers between devices: 78.1 us -> 105 us
  waiting for transfers between devices: 221 us -> 207 us
  other arithmetic: 8.43 us -> 15.8 us
  matrix products: 59 us -> 53.5 us
    unnamed x12 -> x92, local copies, waits for them, and re-layouts: 0.04 us -> 38.2 us
    all_to_all x1 -> x0, blocking collectives: 30.7 us -> none  [forward_transform(): lax.all_to_all(signal.reshape(count, length // count, width).astype(jnp.b...]
    all_to_all x2, waiting for transfers between devices: 24.4 us -> 0.01 us  [forward_transform(): lax.all_to_all(for_sending(mixed_imag), 'seq', split_axis=0, concat_axis=...]
    all_to_all x1 -> x2, starting transfers between devices: 9.78 us -> 26.4 us  [forward_transform(): lax.all_to_all(signal.reshape(count, length // count, width).astype(jnp.b...]
    all_to_all x2, starting transfers between devices: 10.5 us -> 25.1 us  [update_the_cells(): lax.all_to_all(jnp.stack(jnp.split(m, lax.axis_size('seq'), axis=which_di...]
    all_to_all x1 -> x2, waiting for transfers between devices: 9.62 us -> 21.5 us  [forward_transform(): lax.all_to_all(signal.reshape(count, length // count, width).astype(jnp.b...]
    sub x0 -> x2, other arithmetic: none -> 5.45 us  [local_forward(): data_real * cos_t - data_imag * sin_t]
    dot_general x32, matrix products: 47.5 us -> 42.1 us  [apply(): return jnp.einsum(form, left, right, precision=HIGHEST)]
  transfers between devices with their start and end apart: 14 -> 15, of which waited for: 13 -> 12; matrix products, arithmetic and copies ran while one was open for 12% -> 20% of each run, Pallas kernels for 0% -> 0%
where the time goes in v1:
time: 456 us; the launch traced here: 451 us
  waiting for transfers between devices  207 us (45%)
  starting transfers between devices  105 us (23%)
  local copies, waits for them, and re-layouts  55.2 us (12%)
  matrix products  53.5 us (12%)
  other arithmetic  15.8 us (3%)
  between operations  14.7 us (3%)
    reduce_scatter x1, waiting for transfers between devices, per_device(): lax.psum_scatter(partial_sum.astype(jnp.bfloat16), 'tensor', scatter_dime...  55 us
    dot_general x32, matrix products, apply(): return jnp.einsum(form, left, right, precision=HIGHEST)  42.1 us
    psum x1, waiting for transfers between devices, per_device(): lax.psum(result[:, width:].astype(jnp.bfloat16), 'dp').astype(jnp.float32)  41.7 us
    unnamed x92, local copies, waits for them, and re-layouts  38.2 us
    all_to_all x2, starting transfers between devices, forward_transform(): lax.all_to_all(signal.reshape(count, length // count, width).astype(jnp.b...  26.4 us
    all_to_all x2, starting transfers between devices, update_the_cells(): lax.all_to_all(jnp.stack(jnp.split(m, lax.axis_size('seq'), axis=which_di...  25.1 us
    all_to_all x2, waiting for transfers between devices, inverse_transform(): lax.all_to_all(for_sending(data_real), 'seq', split_axis=1, concat_axis=0...  23.4 us
    all_to_all x2, waiting for transfers between devices, inverse_transform(): lax.all_to_all(for_sending(signal), 'seq', split_axis=0, concat_axis=0, t...  23 us
  transfers between devices with their start and end apart: 15, of which 12 were waited for; matrix products, arithmetic and copies ran while one was open for 20% of the time, Pallas kernels for 0%

profile of v1, /device:TPU:1, one launch (start us, length us, event | category | flops | bytes accessed | tf_op | source)
XLA Modules:
  0.0 451.2 jit_solution(15415048442015804878)
XLA Ops:
  9.9 17.2 %all-to-all-start = ((bf16[32,16,256]{2,1,0:T(8,128)(2,1)}), bf16[32,16,256]{2,1,0:T(8,128)(2,1)S(1)}, u32[]{:S(2)}, u32[]{:S(2)}) async-start(bf16[32,16,256]{2,1,0:T(8,128)(2,1)} %bitcast.3), calls=%async_computation | async-start | bytes 524288 | tf_op jit(solution)/shard_map/all_to_all | solution.py:122
  27.9 12.9 %all-to-all-done = bf16[32,16,256]{2,1,0:T(8,128)(2,1)S(1)} async-done(((bf16[32,16,256]{2,1,0:T(8,128)(2,1)}), bf16[32,16,256]{2,1,0:T(8,128)(2,1)S(1)}, u32[]{:S(2)}, u32[]{:S(2)}) %all-to-all-start) | async-done | bytes 262176 | tf_op jit(solution)/shard_map/all_to_all | solution.py:122
  42.6 5.8 %all-to-all-start.2 = ((bf16[64,16,256]{2,1,0:T(8,128)(2,1)}), bf16[64,16,256]{2,1,0:T(8,128)(2,1)S(1)}, u32[]{:S(2)}, u32[]{:S(2)}) async-start(bf16[64,16,256]{2,1,0:T(8,128)(2,1)} %copy.84), calls=%async_computation.2 | async-start | bytes 1048576 | tf_op jit(solution)/shard_map/all_to_all | solution.py:136
  69.1 12.7 %all-to-all-start.1 = ((bf16[32,2,16,256]{3,1,2,0:T(2,128)(2,1)}), bf16[32,2,16,256]{3,1,2,0:T(2,128)(2,1)}, u32[]{:S(2)}, u32[]{:S(2)}) async-start(bf16[32,2,16,256]{3,1,2,0:T(2,128)(2,1)} %constant_dynamic-update-slice_fusion), calls=%async_computation.1 | async-start | bytes 1048576 | tf_op jit(solution)/shard_map/all_to_all | solution.py:13
  84.7 12.9 %all-to-all-done.1 = bf16[32,2,16,256]{3,1,2,0:T(2,128)(2,1)} async-done(((bf16[32,2,16,256]{3,1,2,0:T(2,128)(2,1)}), bf16[32,2,16,256]{3,1,2,0:T(2,128)(2,1)}, u32[]{:S(2)}, u32[]{:S(2)}) %all-to-all-start.1) | async-done | bytes 524320 | tf_op jit(solution)/shard_map/all_to_all | solution.py:13
  114.6 9.2 %all-to-all-start.6 = ((bf16[32,16,128]{2,1,0:T(8,128)(2,1)}), bf16[32,16,128]{2,1,0:T(8,128)(2,1)S(1)}, u32[]{:S(2)}, u32[]{:S(2)}) async-start(bf16[32,16,128]{2,1,0:T(8,128)(2,1)} %bitcast.533), calls=%async_computation.7 | async-start | bytes 262144 | tf_op jit(solution)/shard_map/all_to_all | solution.py:122
  127.7 8.6 %all-to-all-done.6 = bf16[32,16,128]{2,1,0:T(8,128)(2,1)S(1)} async-done(((bf16[32,16,128]{2,1,0:T(8,128)(2,1)}), bf16[32,16,128]{2,1,0:T(8,128)(2,1)S(1)}, u32[]{:S(2)}, u32[]{:S(2)}) %all-to-all-start.6) | async-done | bytes 131104 | tf_op jit(solution)/shard_map/all_to_all | solution.py:122
  137.6 4.6 %all-to-all-start.8 = ((bf16[64,16,128]{2,1,0:T(8,128)(2,1)}), bf16[64,16,128]{2,1,0:T(8,128)(2,1)}, u32[]{:S(2)}, u32[]{:S(2)}) async-start(bf16[64,16,128]{2,1,0:T(8,128)(2,1)} %copy.111), calls=%async_computation.9 | async-start | bytes 524288 | tf_op jit(solution)/shard_map/all_to_all | solution.py:136
  162.1 12.3 %all-to-all-start.7 = ((bf16[32,2,16,128]{3,1,2,0:T(2,128)(2,1)}), bf16[32,2,16,128]{3,1,2,0:T(2,128)(2,1)}, u32[]{:S(2)}, u32[]{:S(2)}) async-start(bf16[32,2,16,128]{3,1,2,0:T(2,128)(2,1)} %constant_dynamic-update-slice_fusion.32), calls=%async_computation.8 | async-start | bytes 524288 | tf_op jit(solution)/shard_map/all_to_all | solution.py:13
  179.6 8.6 %all-to-all-done.7 = bf16[32,2,16,128]{3,1,2,0:T(2,128)(2,1)} async-done(((bf16[32,2,16,128]{3,1,2,0:T(2,128)(2,1)}), bf16[32,2,16,128]{3,1,2,0:T(2,128)(2,1)}, u32[]{:S(2)}, u32[]{:S(2)}) %all-to-all-start.7) | async-done | bytes 262176 | tf_op jit(solution)/shard_map/all_to_all | solution.py:13
  214.8 6.3 %all-to-all-start.10 = ((bf16[2,512,256]{2,0,1:T(2,128)(2,1)}), bf16[2,512,256]{2,0,1:T(2,128)(2,1)S(1)}, u32[]{:S(2)}, u32[]{:S(2)}) async-start(bf16[2,512,256]{2,0,1:T(2,128)(2,1)} %copy.132), calls=%async_computation.11 | async-start | bytes 1048576 | tf_op jit(solution)/shard_map/all_to_all | solution.py:154
  226.3 10.5 %all-to-all-done.10 = bf16[2,512,256]{2,0,1:T(2,128)(2,1)S(1)} async-done(((bf16[2,512,256]{2,0,1:T(2,128)(2,1)}), bf16[2,512,256]{2,0,1:T(2,128)(2,1)S(1)}, u32[]{:S(2)}, u32[]{:S(2)}) %all-to-all-start.10) | async-done | bytes 524320 | tf_op jit(solution)/shard_map/all_to_all | solution.py:154
  236.8 9.3 %all-to-all-start.9 = ((bf16[2,512,256]{2,0,1:T(2,128)(2,1)}), bf16[2,512,256]{2,0,1:T(2,128)(2,1)}, u32[]{:S(2)}, u32[]{:S(2)}) async-start(bf16[2,512,256]{2,0,1:T(2,128)(2,1)} %copy.129), calls=%async_computation.10 | async-start | bytes 1048576 | tf_op jit(solution)/shard_map/all_to_all | solution.py:151
  250.5 11.6 %all-to-all-done.9 = bf16[2,512,256]{2,0,1:T(2,128)(2,1)} async-done(((bf16[2,512,256]{2,0,1:T(2,128)(2,1)}), bf16[2,512,256]{2,0,1:T(2,128)(2,1)}, u32[]{:S(2)}, u32[]{:S(2)}) %all-to-all-start.9) | async-done | bytes 524320 | tf_op jit(solution)/shard_map/all_to_all | solution.py:151
  262.0 9.3 %all-to-all-start.4 = ((bf16[2,512,128]{2,0,1:T(2,128)(2,1)}), bf16[2,512,128]{2,0,1:T(2,128)(2,1)S(1)}, u32[]{:S(2)}, u32[]{:S(2)}) async-start(bf16[2,512,128]{2,0,1:T(2,128)(2,1)} %copy.105), calls=%async_computation.4 | async-start | bytes 524288 | tf_op jit(solution)/shard_map/all_to_all | solution.py:154
  275.0 9.9 %all-to-all-done.4 = bf16[2,512,128]{2,0,1:T(2,128)(2,1)S(1)} async-done(((bf16[2,512,128]{2,0,1:T(2,128)(2,1)}), bf16[2,512,128]{2,0,1:T(2,128)(2,1)S(1)}, u32[]{:S(2)}, u32[]{:S(2)}) %all-to-all-start.4) | async-done | bytes 262176 | tf_op jit(solution)/shard_map/all_to_all | solution.py:154
  284.9 5.8 %all-to-all-start.3 = ((bf16[2,512,128]{2,0,1:T(2,128)(2,1)}), bf16[2,512,128]{2,0,1:T(2,128)(2,1)S(1)}, u32[]{:S(2)}, u32[]{:S(2)}) async-start(bf16[2,512,128]{2,0,1:T(2,128)(2,1)} %copy.102), calls=%async_computation.3 | async-start | bytes 524288 | tf_op jit(solution)/shard_map/all_to_all | solution.py:151
  292.5 11.9 %all-to-all-done.3 = bf16[2,512,128]{2,0,1:T(2,128)(2,1)S(1)} async-done(((bf16[2,512,128]{2,0,1:T(2,128)(2,1)}), bf16[2,512,128]{2,0,1:T(2,128)(2,1)S(1)}, u32[]{:S(2)}, u32[]{:S(2)}) %all-to-all-start.3) | async-done | bytes 262176 | tf_op jit(solution)/shard_map/all_to_all | solution.py:151
  304.4 6.1 %all-to-all-start.11 = ((bf16[32,16,256]{2,1,0:T(8,128)(2,1)}), bf16[32,16,256]{2,1,0:T(8,128)(2,1)S(1)}, u32[]{:S(2)}, u32[]{:S(2)}) async-start(bf16[32,16,256]{2,1,0:T(8,128)(2,1)} %copy.135), calls=%async_computation.12 | async-start | bytes 524288 | tf_op jit(solution)/shard_map/all_to_all | solution.py:165
  312.6 11.5 %all-to-all-done.11 = bf16[32,16,256]{2,1,0:T(8,128)(2,1)S(1)} async-done(((bf16[32,16,256]{2,1,0:T(8,128)(2,1)}), bf16[32,16,256]{2,1,0:T(8,128)(2,1)S(1)}, u32[]{:S(2)}, u32[]{:S(2)}) %all-to-all-start.11) | async-done | bytes 262176 | tf_op jit(solution)/shard_map/all_to_all | solution.py:165
  324.0 5.8 %all-to-all-start.5 = ((bf16[32,16,128]{2,1,0:T(8,128)(2,1)}), bf16[32,16,128]{2,1,0:T(8,128)(2,1)S(1)}, u32[]{:S(2)}, u32[]{:S(2)}) async-start(bf16[32,16,128]{2,1,0:T(8,128)(2,1)} %copy.108), calls=%async_computation.5 | async-start | bytes 262144 | tf_op jit(solution)/shard_map/all_to_all | solution.py:165
  330.7 11.5 %all-to-all-done.5 = bf16[32,16,128]{2,1,0:T(8,128)(2,1)S(1)} async-done(((bf16[32,16,128]{2,1,0:T(8,128)(2,1)}), bf16[32,16,128]{2,1,0:T(8,128)(2,1)S(1)}, u32[]{:S(2)}, u32[]{:S(2)}) %all-to-all-start.5) | async-done | bytes 131104 | tf_op jit(solution)/shard_map/all_to_all | solution.py:165
  346.2 41.7 %all-reduce.2.cloned.1.call-done = bf16[512,128]{1,0:T(8,128)(2,1)} async-done(((bf16[512,128]{1,0:T(8,128)(2,1)}), bf16[512,128]{1,0:T(8,128)(2,1)}) %all-reduce.2.cloned.1.call-update) | async-done | bytes 131088 | tf_op jit(solution)/shard_map/psum | solution.py:215
  389.5 55.0 %reduce-scatter.2.cloned.1.call-done = bf16[512,1024]{1,0:T(8,128)(2,1)} async-done(((bf16[512,4096]{1,0:T(8,128)(2,1)}), bf16[512,1024]{1,0:T(8,128)(2,1)}) %reduce-scatter.2.cloned.1.call-update) | async-done | bytes 1048592 | tf_op jit(solution)/shard_map/reduce_scatter | solution.py:195
  (185 shorter events, 125.4 us)
Async XLA Ops:
  7.2 103.3 %copy-start = (bf16[128,4096]{1,0:T(8,128)(2,1)S(1)}, bf16[128,4096]{1,0:T(8,128)(2,1)}, u32[]{:S(2)}) copy-start(bf16[128,4096]{1,0:T(8,128)(2,1)} %param.8) | copy-start | bytes 3145732
  9.9 30.9 %all-to-all-start = ((bf16[32,16,256]{2,1,0:T(8,128)(2,1)}), bf16[32,16,256]{2,1,0:T(8,128)(2,1)S(1)}, u32[]{:S(2)}, u32[]{:S(2)}) async-start(bf16[32,16,256]{2,1,0:T(8,128)(2,1)} %bitcast.3), calls=%async_computation | async-start | bytes 524288 | tf_op jit(solution)/shard_map/all_to_all | solution.py:122
  27.1 83.3 %all-gather.3.cloned.1.call-start = ((), (), s32[]{:S(2)}) async-start(), calls=%async_computation.15 | async-start | bytes 5242880 | tf_op jit(solution)/shard_map/all_gather | solution.py:199
  42.6 26.5 %all-to-all-start.2 = ((bf16[64,16,256]{2,1,0:T(8,128)(2,1)}), bf16[64,16,256]{2,1,0:T(8,128)(2,1)S(1)}, u32[]{:S(2)}, u32[]{:S(2)}) async-start(bf16[64,16,256]{2,1,0:T(8,128)(2,1)} %copy.84), calls=%async_computation.2 | async-start | bytes 1048576 | tf_op jit(solution)/shard_map/all_to_all | solution.py:136
  69.1 28.5 %all-to-all-start.1 = ((bf16[32,2,16,256]{3,1,2,0:T(2,128)(2,1)}), bf16[32,2,16,256]{3,1,2,0:T(2,128)(2,1)}, u32[]{:S(2)}, u32[]{:S(2)}) async-start(bf16[32,2,16,256]{3,1,2,0:T(2,128)(2,1)} %constant_dynamic-update-slice_fusion), calls=%async_computation.1 | async-start | bytes 1048576 | tf_op jit(solution)/shard_map/all_to_all | solution.py:13
  84.5 19.5 %copy-start.1 = (f32[2,32,16]{0,2,1:T(8,128)}, f32[2,32,16]{0,2,1:T(8,128)S(1)}, u32[]{:S(2)}) copy-start(f32[2,32,16]{0,2,1:T(8,128)S(1)} %get-tuple-element.29) | copy-start | bytes 12292
  100.5 5.2 %copy-start.8 = (f32[32,16]{0,1:T(8,128)S(1)}, f32[32,16]{0,1:T(8,128)}, u32[]{:S(2)}) copy-start(f32[32,16]{0,1:T(8,128)} %copy-done.7) | copy-start | bytes 6148
  100.5 5.2 %copy-start.11 = (f32[32,16]{0,1:T(8,128)S(1)}, f32[32,16]{0,1:T(8,128)}, u32[]{:S(2)}) copy-start(f32[32,16]{0,1:T(8,128)} %copy-done.10) | copy-start | bytes 6148
  105.7 4.7 %copy-start.4 = (bf16[1,512,128]{2,1,0:T(8,128)(2,1)S(1)}, bf16[1,512,128]{2,1,0:T(8,128)(2,1)}, u32[]{:S(2)}) copy-start(bf16[1,512,128]{2,1,0:T(8,128)(2,1)} %param.5) | copy-start | bytes 393220
  114.6 21.6 %all-to-all-start.6 = ((bf16[32,16,128]{2,1,0:T(8,128)(2,1)}), bf16[32,16,128]{2,1,0:T(8,128)(2,1)S(1)}, u32[]{:S(2)}, u32[]{:S(2)}) async-start(bf16[32,16,128]{2,1,0:T(8,128)(2,1)} %bitcast.533), calls=%async_computation.7 | async-start | bytes 262144 | tf_op jit(solution)/shard_map/all_to_all | solution.py:122
  137.6 24.5 %all-to-all-start.8 = ((bf16[64,16,128]{2,1,0:T(8,128)(2,1)}), bf16[64,16,128]{2,1,0:T(8,128)(2,1)}, u32[]{:S(2)}, u32[]{:S(2)}) async-start(bf16[64,16,128]{2,1,0:T(8,128)(2,1)} %copy.111), calls=%async_computation.9 | async-start | bytes 524288 | tf_op jit(solution)/shard_map/all_to_all | solution.py:136
  162.1 26.0 %all-to-all-start.7 = ((bf16[32,2,16,128]{3,1,2,0:T(2,128)(2,1)}), bf16[32,2,16,128]{3,1,2,0:T(2,128)(2,1)}, u32[]{:S(2)}, u32[]{:S(2)}) async-start(bf16[32,2,16,128]{3,1,2,0:T(2,128)(2,1)} %constant_dynamic-update-slice_fusion.32), calls=%async_computation.8 | async-start | bytes 524288 | tf_op jit(solution)/shard_map/all_to_all | solution.py:13
  177.7 15.8 %copy-start.9 = (f32[32,16]{0,1:T(8,128)S(1)}, f32[32,16]{0,1:T(8,128)}, u32[]{:S(2)}) copy-start(f32[32,16]{0,1:T(8,128)} %copy-done.7) | copy-start | bytes 6148
  177.8 15.8 %copy-start.12 = (f32[32,16]{0,1:T(8,128)S(1)}, f32[32,16]{0,1:T(8,128)}, u32[]{:S(2)}) copy-start(f32[32,16]{0,1:T(8,128)} %copy-done.10) | copy-start | bytes 6148
  192.5 4.8 %copy-start.2 = (f32[2,32,16,256]{3,2,1,0:T(8,128)S(1)}, f32[2,32,16,256]{3,2,1,0:T(8,128)}, u32[]{:S(2)}) copy-start(f32[2,32,16,256]{3,2,1,0:T(8,128)} %fusion.5) | copy-start | bytes 3145732
  214.8 22.0 %all-to-all-start.10 = ((bf16[2,512,256]{2,0,1:T(2,128)(2,1)}), bf16[2,512,256]{2,0,1:T(2,128)(2,1)S(1)}, u32[]{:S(2)}, u32[]{:S(2)}) async-start(bf16[2,512,256]{2,0,1:T(2,128)(2,1)} %copy.132), calls=%async_computation.11 | async-start | bytes 1048576 | tf_op jit(solution)/shard_map/all_to_all | solution.py:154
  236.8 25.2 %all-to-all-start.9 = ((bf16[2,512,256]{2,0,1:T(2,128)(2,1)}), bf16[2,512,256]{2,0,1:T(2,128)(2,1)}, u32[]{:S(2)}, u32[]{:S(2)}) async-start(bf16[2,512,256]{2,0,1:T(2,128)(2,1)} %copy.129), calls=%async_computation.10 | async-start | bytes 1048576 | tf_op jit(solution)/shard_map/all_to_all | solution.py:151
  262.0 22.9 %all-to-all-start.4 = ((bf16[2,512,128]{2,0,1:T(2,128)(2,1)}), bf16[2,512,128]{2,0,1:T(2,128)(2,1)S(1)}, u32[]{:S(2)}, u32[]{:S(2)}) async-start(bf16[2,512,128]{2,0,1:T(2,128)(2,1)} %copy.105), calls=%async_computation.4 | async-start | bytes 524288 | tf_op jit(solution)/shard_map/all_to_all | solution.py:154
  275.0 67.3 %copy-start.5 = (bf16[1,512,128]{2,1,0:T(8,128)(2,1)S(1)}, bf16[1,512,128]{2,1,0:T(8,128)(2,1)}, u32[]{:S(2)}) copy-start(bf16[1,512,128]{2,1,0:T(8,128)(2,1)} %param.5) | copy-start | bytes 393220
  284.9 19.5 %all-to-all-start.3 = ((bf16[2,512,128]{2,0,1:T(2,128)(2,1)}), bf16[2,512,128]{2,0,1:T(2,128)(2,1)S(1)}, u32[]{:S(2)}, u32[]{:S(2)}) async-start(bf16[2,512,128]{2,0,1:T(2,128)(2,1)} %copy.102), calls=%async_computation.3 | async-start | bytes 524288 | tf_op jit(solution)/shard_map/all_to_all | solution.py:151
  304.4 19.6 %all-to-all-start.11 = ((bf16[32,16,256]{2,1,0:T(8,128)(2,1)}), bf16[32,16,256]{2,1,0:T(8,128)(2,1)S(1)}, u32[]{:S(2)}, u32[]{:S(2)}) async-start(bf16[32,16,256]{2,1,0:T(8,128)(2,1)} %copy.135), calls=%async_computation.12 | async-start | bytes 524288 | tf_op jit(solution)/shard_map/all_to_all | solution.py:165
  324.0 18.2 %all-to-all-start.5 = ((bf16[32,16,128]{2,1,0:T(8,128)(2,1)}), bf16[32,16,128]{2,1,0:T(8,128)(2,1)S(1)}, u32[]{:S(2)}, u32[]{:S(2)}) async-start(bf16[32,16,128]{2,1,0:T(8,128)(2,1)} %copy.108), calls=%async_computation.5 | async-start | bytes 262144 | tf_op jit(solution)/shard_map/all_to_all | solution.py:165
  329.9 58.0 %all-reduce.2.cloned.1.call-start = ((), (), s32[]{:S(2)}) async-start(), calls=%async_computation.14 | async-start | bytes 262144 | tf_op jit(solution)/shard_map/psum | solution.py:215
  330.7 113.8 %reduce-scatter.2.cloned.1.call-start = ((), (), s32[]{:S(2)}) async-start(), calls=%async_computation.13 | async-start | bytes 5242880 | tf_op jit(solution)/shard_map/reduce_scatter | solution.py:195
  (6 other events, 14.7 us)
Sparse Core Ops, SparseCore 0:
  30.1 53.9 all-gather.2
  333.6 54.1 all-reduce.1
  391.5 52.8 reduce-scatter.1
